TPU v7x, 32 devices: a whole 2x2x4 slice. The times are simulated.
32 devices in a mesh: scene: 2 (over y), bins: 4 (over z), az: 4 (over x, core).
Axes of the slice: x: 2, y: 2, z: 4, core: 2. Of those that a mesh axis runs over, the one named last changes fastest.
Arguments:
- raw_echoes: bfloat16 [2, 8, 512, 16384], P(None, ('scene', 'az'), 'bins'), parts along dimension 1, may hold values from -6 to 6
- range_phase: float32 [16384], replicated, may hold values from -3.140625 to 3.140625
- band_start: int32 [16384], replicated, may hold values from 0 to 16447, as said below
- band_weight: bfloat16 [8, 16384], replicated, may hold values from -0.25 to 0.75
- intersection_length: int32 [16384], P('bins'), may hold values from 32 to 128
- azimuth_rate: float32 [16384], P('bins'), may hold values from 0.25 to 2
Outputs:
- focused_image: bfloat16 [2, 8, 512, 16384], P(None, ('scene', 'az'), None, 'bins'), parts along dimension 1
There are 2 independent parts, one for each index of `scene`. A program takes and returns all parts, laid end to end along the dimension named above; an argument that names none is the same for every part. Nothing has to cross between parts.
Inputs may be any that keep to these rules, and one draw needn't show every extreme that they name: band_start[b] - b lies between 0 and 64 for every range bin b.
All inputs are finite; a program needn't handle non-finite values.
Results may differ from a plain program's by a relative error of at most 0.02.
Values may be sent and summed in bfloat16 or wider, within the bound.
A program may use at most 128 MiB of HBM per device.

v0:
```python
import math

import jax
import jax.numpy as jnp
from jax import lax
from jax.sharding import PartitionSpec as P

OVLMAX = 128


def passed_along(value, axis, steps):
    count = lax.axis_size(axis)
    first, last = (max(0, -steps), min(count, count - steps))
    return lax.ppermute(value, axis, [(source, source + steps) for source in range(first, last)])


def phase_pair(row_count, col_count, length, direction):
    row_index = jnp.arange(row_count, dtype=jnp.int32)[:, None]
    col_index = jnp.arange(col_count, dtype=jnp.int32)[None, :]
    product = (row_index * col_index % length).astype(jnp.float32)
    phase_angle = product * (direction * 2.0 * math.pi / length)
    return (jnp.cos(phase_angle), jnp.sin(phase_angle))


def narrow_pair(operands):
    return (operands[0].astype(jnp.bfloat16), operands[1].astype(jnp.bfloat16))


def complex_product(form, left_pair, right_pair):
    left_real, left_imag = left_pair
    right_real, right_imag = right_pair
    real_part = jnp.einsum(
        form, left_real, right_real, preferred_element_type=jnp.float32
    ) - jnp.einsum(form, left_imag, right_imag, preferred_element_type=jnp.float32)
    imag_part = jnp.einsum(
        form, left_real, right_imag, preferred_element_type=jnp.float32
    ) + jnp.einsum(form, left_imag, right_real, preferred_element_type=jnp.float32)
    return (real_part, imag_part)


def complex_scale(operands, cosine, sine_part):
    real_part = operands[0] * cosine - operands[1] * sine_part
    imag_part = operands[0] * sine_part + operands[1] * cosine
    return (real_part, imag_part)


def compress_lines(echo_lines, range_phase):
    line_count, line_width = (echo_lines.shape[1], echo_lines.shape[2])
    radix_size = 128
    other_size = line_width // radix_size
    line_grid = echo_lines.reshape(2, line_count, radix_size, other_size)
    first_table = narrow_pair(phase_pair(radix_size, radix_size, radix_size, -1.0))
    partial_value = complex_product("ka,pan->pkn", first_table, (line_grid[0], line_grid[1]))
    partial_value = complex_scale(
        partial_value, *phase_pair(radix_size, other_size, line_width, -1.0)
    )
    second_table = narrow_pair(phase_pair(other_size, other_size, other_size, -1.0))
    spectrum = complex_product("pkn,nm->pkm", narrow_pair(partial_value), second_table)
    filter_angle = range_phase.reshape(other_size, radix_size).T
    filtered = narrow_pair(complex_scale(spectrum, jnp.cos(filter_angle), -jnp.sin(filter_angle)))
    back_table = narrow_pair(phase_pair(other_size, other_size, other_size, 1.0))
    partial_value = complex_product("pkm,mn->pkn", filtered, back_table)
    partial_value = complex_scale(
        partial_value, *phase_pair(radix_size, other_size, line_width, 1.0)
    )
    last_table = narrow_pair(phase_pair(radix_size, radix_size, radix_size, 1.0))
    result = complex_product("ak,pkn->pan", last_table, narrow_pair(partial_value))
    stacked = jnp.stack(result) * (1.0 / line_width)
    return stacked.reshape(2, line_count, line_width).astype(jnp.bfloat16)


def migrate(samples, range_rim, starts, weights):
    row_count, line_width = (samples.shape[1], samples.shape[2])
    blocks = line_width // 128
    extended = jnp.concatenate([samples, range_rim], axis=2)
    windows = jnp.concatenate(
        [
            extended[:, :, :line_width].reshape(2, row_count, blocks, 128),
            extended[:, :, 128:].reshape(2, row_count, blocks, 128),
        ],
        axis=3,
    )
    block_start = 128 * jnp.arange(blocks, dtype=jnp.int32)[:, None]
    offsets = starts.reshape(blocks, 128) - block_start
    position = jnp.arange(256, dtype=jnp.int32)[None, :, None]
    band_matrix = jnp.zeros((blocks, 256, 128), jnp.bfloat16)
    for tap_index in range(weights.shape[0]):
        tap_weight = weights[tap_index].reshape(blocks, 128)[:, None, :]
        band_matrix = band_matrix + jnp.where(
            position == (offsets + tap_index)[:, None, :], tap_weight, jnp.zeros((), jnp.bfloat16)
        )
    result = jnp.einsum("sprj,rjk->sprk", windows, band_matrix, preferred_element_type=jnp.float32)
    return result.reshape(2, row_count, line_width).astype(jnp.bfloat16)


def shards(raw_echoes, range_phase, band_start, band_weight, intersection_length, azimuth_rate):
    echo_lines = raw_echoes[:, 0]
    compressed = compress_lines(echo_lines, range_phase)
    empty_rim = jnp.zeros((2, compressed.shape[1], 128), jnp.bfloat16)
    outgoing = migrate(compressed, empty_rim, band_start, band_weight)
    turned = lax.all_to_all(outgoing, "bins", split_axis=2, concat_axis=1, tiled=True)
    head_lines = passed_along(turned[:, :OVLMAX], "az", -1)
    aperture = jnp.concatenate([turned, head_lines], axis=1)
    own_count = turned.shape[1]
    length = aperture.shape[1]
    pulses = jnp.arange(length, dtype=jnp.int32)[:, None]
    inside = (pulses < own_count) | (pulses - own_count < intersection_length[None, :])
    aperture = jnp.where(inside[None], aperture, jnp.zeros((), jnp.bfloat16))
    forward_table = narrow_pair(phase_pair(length, length, length, -1.0))
    spectrum = complex_product("fp,pr->fr", forward_table, (aperture[0], aperture[1]))
    doppler = jnp.arange(length, dtype=jnp.int32)
    signed = jnp.where(2 * doppler >= length, doppler - length, doppler).astype(jnp.float32)
    phase_angle = math.pi * azimuth_rate[None, :] * (signed * signed)[:, None] / length
    focused = narrow_pair(complex_scale(spectrum, jnp.cos(phase_angle), -jnp.sin(phase_angle)))
    inverse_table = narrow_pair(phase_pair(own_count, length, length, 1.0))
    image_pair = complex_product("qf,fr->qr", inverse_table, focused)
    stacked = jnp.stack(image_pair) * (1.0 / length)
    return stacked.astype(jnp.bfloat16)[:, None]


def solution(mesh):
    in_specs = (P(None, ("scene", "az"), "bins", None), P(), P(), P(), P("bins"), P("bins"))
    out_specs = P(None, ("scene", "az"), None, "bins")
    return jax.shard_map(shards, mesh=mesh, in_specs=in_specs, out_specs=out_specs, check_vma=False)
```

profile of v0, /device:TPU:9, one launch (start us, length us, event | category | flops | bytes accessed | tf_op | source)
XLA Modules:
  0.0 639.4 jit_solution(2054546862084710419)
XLA Ops:
  20.9 10.6 %fusion.42 = (bf16[128,128,128]{2,1,0:T(8,128)(2,1)S(1)}, bf16[128,128,128]{2,1,0:T(8,128)(2,1)S(1)}) fusion(f32[128,128]{1,0:T(8,128)S(1)} %get-tuple-element.37, f32[128,128]{1,0:T(8,128)S(1)} %get-tuple-element.38, f32[128,128,128]{2,0,1:T(8,128)} %fusion.105, f32[128,128,128]{2,0,1:T(8,128)} %fusion.97, f32[128,128,128]{2,0,1:T(8,128)} %fusion.99, ...), kind=kOutput, calls=%fused_computation.64 | convolution fusion | flops 558088192 | bytes 37879808 | tf_op jit(solution)/shard_map/ka,pan->pkn/dot_general | solution.py:32
  46.2 13.0 %add_convert_fusion.2 = (bf16[128,128,128]{2,1,0:T(8,128)(2,1)S(1)}, bf16[128,128,128]{2,1,0:T(8,128)(2,1)S(1)}) fusion(f32[128,128]{1,0:T(8,128)S(1)} %copy.36, f32[128,128]{1,0:T(8,128)S(1)} %copy.35, f32[128,128,128]{2,1,0:T(8,128)} %fusion.101, f32[128,128,128]{2,1,0:T(8,128)} %fusion.103, f32[128,128,128]{2,1,0:T(8,128)} %fusion.95, ...), kind=kOutput, calls=%fused_computation.45 | convolution fusion | flops 558088192 | bytes 37879808 | tf_op jit(solution)/shard_map/pkn,nm->pkm/dot_general | solution.py:35
  73.8 12.9 %subtract_convert_fusion.1 = (bf16[128,128,128]{2,1,0:T(8,128)(2,1)}, bf16[128,128,128]{2,1,0:T(8,128)(2,1)S(1)}) fusion(f32[128,128]{1,0:T(8,128)S(1)} %get-tuple-element.39, f32[128,128]{1,0:T(8,128)S(1)} %get-tuple-element.40, f32[128,128,128]{2,1,0:T(8,128)} %fusion.89, f32[128,128,128]{2,1,0:T(8,128)} %fusion.91, f32[128,128,128]{2,1,0:T(8,128)} %fusion.83, ...), kind=kOutput, calls=%fused_computation.44 | convolution fusion | flops 558088192 | bytes 37879808 | tf_op jit(solution)/shard_map/pkm,mn->pkn/dot_general | solution.py:35
  93.1 10.6 %subtract_bitcast_fusion.1 = (f32[1,128,128,128]{2,3,1,0:T(8,128)}, f32[128,128,128]{1,2,0:T(8,128)}) fusion(f32[128,128,128]{2,1,0:T(8,128)} %fusion.79, bf16[128,128,128]{2,1,0:T(8,128)(2,1)S(1)} %copy-done.1), kind=kOutput, calls=%fused_computation.78 | convolution fusion | flops 539213824 | bytes 29360128 | tf_op jit(solution)/shard_map/ak,pkn->pan/dot_general | solution.py:32
  111.2 9.4 %copy.41 = f32[128,128,128]{0,2,1:T(8,128)} copy(f32[128,128,128]{1,2,0:T(8,128)} %get-tuple-element.24) | data formatting | bytes 16777216 | tf_op jit(solution)/shard_map/sub | solution.py:32
  120.6 9.4 %copy.42 = f32[128,128,128]{0,2,1:T(8,128)} copy(f32[128,128,128]{1,2,0:T(8,128)} %get-tuple-element.26) | data formatting | bytes 16777216 | tf_op jit(solution)/shard_map/add | solution.py:35
  140.4 13.6 %copy.43 = bf16[2,128,128,128]{2,3,1,0:T(8,128)(2,1)} copy(bf16[2,128,128,128]{1,3,2,0:T(8,128)(2,1)} %bitcast.147) | data formatting | bytes 16777216 | tf_op jit(solution)/shard_map/reshape | solution.py:79
  168.7 23.6 %copy.44 = bf16[2,128,128,256]{3,1,0,2:T(8,128)(2,1)} copy(bf16[2,128,128,256]{2,3,1,0:T(8,128)(2,1)} %pad_maximum_fusion) | data formatting | bytes 33554432 | tf_op jit(solution)/shard_map/concatenate | solution.py:76
  193.9 38.2 %fusion.232 = bf16[128,256,128,1]{1,2,3,0:T(8,128)(2,1)} fusion(s32[128,128]{1,0:T(8,128)S(1)} %get-tuple-element.34, s32[128,128]{1,0:T(8,128)S(1)} %get-tuple-element.30, s32[128,128]{1,0:T(8,128)S(1)} %get-tuple-element.31, s32[128,128]{1,0:T(8,128)S(1)} %get-tuple-element.32, s32[128,128]{1,0:T(8,128)S(1)} %get-tuple-element.33, ...), kind=kLoop, calls=%fused_computation.32.clone.clone.clone.clone.1 | loop fusion | flops 134217728 | bytes 9175040 | tf_op jit(solution)/shard_map/sprj,rjk->sprk/dot_general | solution.py:92
  232.1 13.1 %convert_bitcast_fusion = bf16[2,128,128,128]{1,3,0,2:T(8,128)(2,1)} fusion(bf16[2,128,128,256]{3,1,0,2:T(8,128)(2,1)} %copy.44, bf16[128,256,128,1]{1,2,3,0:T(8,128)(2,1)} %fusion.232), kind=kOutput, calls=%fused_computation.42 | convolution fusion | flops 2151677952 | bytes 33554432 | tf_op jit(solution)/shard_map/sprj,rjk->sprk/dot_general | solution.py:92
  245.2 10.5 %copy.45 = bf16[2,128,128,128]{1,3,2,0:T(8,128)(2,1)} copy(bf16[2,128,128,128]{1,3,0,2:T(8,128)(2,1)} %convert_bitcast_fusion) | data formatting | bytes 16777216 | tf_op jit(solution)/shard_map/convert_element_type | solution.py:93
  255.7 15.6 %copy.46 = bf16[2,128,16384]{1,0,2:T(2,128)(2,1)S(1)} copy(bf16[2,128,16384]{1,2,0:T(8,128)(2,1)} %bitcast.148) | data formatting | bytes 16777216 | tf_op jit(solution)/shard_map/convert_element_type | solution.py:93
  271.3 184.9 %all_to_all.18 = bf16[2,128,16384]{1,0,2:T(2,128)(2,1)S(1)} all-to-all(bf16[2,128,16384]{1,0,2:T(2,128)(2,1)S(1)} %copy.46), channel_id=1, replica_groups=mesh['scene'=2,'bins'=4,'az'=4] {'bins'}, dimensions={2} | all-to-all | bytes 16777216 | tf_op jit(solution)/shard_map/all_to_all | solution.py:101
  456.2 10.5 %copy.47 = bf16[2,128,16384]{1,2,0:T(8,128)(2,1)} copy(bf16[2,128,16384]{1,0,2:T(2,128)(2,1)S(1)} %all_to_all.18) | data formatting | bytes 16777216 | tf_op jit(solution)/shard_map/all_to_all | solution.py:101
  466.7 12.1 %copy.48 = bf16[2,4,128,4096]{3,2,1,0:T(8,128)(2,1)} copy(bf16[2,4,128,4096]{2,3,1,0:T(8,128)(2,1)} %bitcast.149) | data formatting | bytes 16777216 | tf_op jit(solution)/shard_map/all_to_all | solution.py:101
  493.6 15.8 %collective-permute-done = bf16[2,128,4096]{2,1,0:T(8,128)(2,1)S(1)} collective-permute-done((bf16[2,128,4096]{2,1,0:T(8,128)(2,1)S(1)}, bf16[2,128,4096]{2,1,0:T(8,128)(2,1)S(1)}, u32[]{:S(2)}, u32[]{:S(2)}) %collective-permute-start) | collective-permute-done | bytes 2097184 | tf_op jit(solution)/shard_map/ppermute | solution.py:14
  517.3 12.6 %fusion.40 = f32[640,4096]{1,0:T(8,128)} fusion(bf16[2,640,4096]{2,1,0:T(8,128)(2,1)S(1)} %maximum_select_fusion), kind=kOutput, calls=%fused_computation.62 | convolution fusion | flops 3359539200 | bytes 15728640 | tf_op jit(solution)/shard_map/fp,pr->fr/dot_general | solution.py:34
  529.9 12.9 %fusion.39 = f32[640,4096]{1,0:T(8,128)} fusion(bf16[2,640,4096]{2,1,0:T(8,128)(2,1)S(1)} %maximum_select_fusion), kind=kOutput, calls=%fused_computation.61 | convolution fusion | flops 3359539200 | bytes 15728640 | tf_op jit(solution)/shard_map/fp,pr->fr/dot_general | solution.py:37
  542.8 12.9 %convolution_subtract_fusion = f32[640,4096]{1,0:T(8,128)S(1)} fusion(f32[640,4096]{1,0:T(8,128)} %fusion.40, bf16[2,640,4096]{2,1,0:T(8,128)(2,1)S(1)} %maximum_select_fusion), kind=kOutput, calls=%fused_computation.58 | convolution fusion | flops 3362160640 | bytes 26214400 | tf_op jit(solution)/shard_map/fp,pr->fr/dot_general | solution.py:32
  555.7 46.4 %subtract_convert_fusion = (bf16[640,4096]{1,0:T(8,128)(2,1)S(1)}, bf16[640,4096]{1,0:T(8,128)(2,1)}) fusion(f32[640,4096]{1,0:T(8,128)S(1)} %convolution_subtract_fusion, f32[640]{0:T(1024)S(1)} %fusion.111, f32[4096]{0:T(1024)S(1)} %broadcast_multiply_fusion, f32[640,4096]{1,0:T(8,128)} %fusion.39, bf16[2,640,4096]{2,1,0:T(8,128)(2,1)S(1)} %maximum_select_fusion, ...), kind=kOutput, calls=%fused_computation.25 | convolution fusion | flops 3386900480 | bytes 37539840 | tf_op jit(solution)/shard_map/fp,pr->fr/dot_general | solution.py:35
  602.2 8.0 %fusion.63 = f32[512,4096]{1,0:T(8,128)S(1)} fusion(bf16[640,4096]{1,0:T(8,128)(2,1)S(1)} %get-tuple-element.21), kind=kOutput, calls=%fused_computation.99 | convolution fusion | flops 2687631360 | bytes 13631488 | tf_op jit(solution)/shard_map/qf,fr->qr/dot_general | solution.py:32
  610.3 8.4 %fusion.62 = f32[512,4096]{1,0:T(8,128)S(1)} fusion(bf16[640,4096]{1,0:T(8,128)(2,1)S(1)} %bitcast.159), kind=kOutput, calls=%fused_computation.98 | convolution fusion | flops 2687631360 | bytes 13631488 | tf_op jit(solution)/shard_map/qf,fr->qr/dot_general | solution.py:35
  618.7 8.1 %subtract_bitcast_fusion = f32[1,1,512,4096]{3,2,1,0:T(8,128)S(1)} fusion(f32[512,4096]{1,0:T(8,128)S(1)} %fusion.63, bf16[640,4096]{1,0:T(8,128)(2,1)S(1)} %bitcast.159), kind=kOutput, calls=%fused_computation.41 | convolution fusion | flops 2689728512 | bytes 22020096 | tf_op jit(solution)/shard_map/qf,fr->qr/dot_general | solution.py:34
  626.8 8.3 %add_bitcast_fusion = f32[1,1,512,4096]{3,2,1,0:T(8,128)S(1)} fusion(f32[512,4096]{1,0:T(8,128)S(1)} %fusion.62, bf16[640,4096]{1,0:T(8,128)(2,1)S(1)} %copy-done.9), kind=kOutput, calls=%fused_computation.40 | convolution fusion | flops 2689728512 | bytes 22020096 | tf_op jit(solution)/shard_map/qf,fr->qr/dot_general | solution.py:37
  (63 shorter events, 117.3 us)
Async XLA Ops:
  31.5 9.6 %copy-start = (bf16[128,128,128]{2,1,0:T(8,128)(2,1)}, bf16[128,128,128]{2,1,0:T(8,128)(2,1)S(1)}, u32[]{:S(2)}) copy-start(bf16[128,128,128]{2,1,0:T(8,128)(2,1)S(1)} %get-tuple-element.20) | copy-start | bytes 12582916
  41.1 4.7 copy-start.4
  86.7 4.9 copy-start.1
  154.0 8.2 %copy-start.2 = (bf16[2,128,128,128]{2,3,1,0:T(8,128)(2,1)S(1)}, bf16[2,128,128,128]{2,3,1,0:T(8,128)(2,1)}, u32[]{:S(2)}) copy-start(bf16[2,128,128,128]{2,3,1,0:T(8,128)(2,1)} %copy.43) | copy-start | bytes 25165828
  168.7 23.7 %copy-start.5 = (s32[16384]{0:T(1024)S(1)}, s32[16384]{0:T(1024)}, u32[]{:S(2)}) copy-start(s32[16384]{0:T(1024)} %param.8) | copy-start | bytes 196612
  168.7 23.8 %copy-start.3 = (bf16[8,16384]{1,0:T(8,128)(2,1)S(1)}, bf16[8,16384]{1,0:T(8,128)(2,1)}, u32[]{:S(2)}) copy-start(bf16[8,16384]{1,0:T(8,128)(2,1)} %param.9) | copy-start | bytes 786436
  466.7 24.4 %copy-start.7 = (f32[4096]{0:T(1024)S(1)}, f32[4096]{0:T(1024)}, u32[]{:S(2)}) copy-start(f32[4096]{0:T(1024)} %param.11) | copy-start | bytes 49156
  466.7 24.5 %copy-start.6 = (s32[4096]{0:T(1024)S(1)}, s32[4096]{0:T(1024)}, u32[]{:S(2)}) copy-start(s32[4096]{0:T(1024)} %param.10) | copy-start | bytes 49156
  480.6 28.8 %collective-permute-start = (bf16[2,128,4096]{2,1,0:T(8,128)(2,1)S(1)}, bf16[2,128,4096]{2,1,0:T(8,128)(2,1)S(1)}, u32[]{:S(2)}, u32[]{:S(2)}) collective-permute-start(bf16[2,128,4096]{2,1,0:T(8,128)(2,1)S(1)} %slice.58), channel_id=1, source_target_pairs={{1,0},{2,1},{3,2},{5,4},{6,5},{7,6},{9,8},{10,9},{11,10},{13,12},{... | collective-permute-start | bytes 6291464 | tf_op jit(solution)/shard_map/ppermute | solution.py:14
  602.2 8.1 %copy-start.8 = (bf16[640,4096]{1,0:T(8,128)(2,1)}, bf16[640,4096]{1,0:T(8,128)(2,1)S(1)}, u32[]{:S(2)}) copy-start(bf16[640,4096]{1,0:T(8,128)(2,1)S(1)} %get-tuple-element.21) | copy-start | bytes 15728644
  602.2 8.1 %slice-start = ((s8[5242880]{0:T(1024)(128)(4,1)}), s8[4194304]{0:T(1024)(128)(4,1)S(1)}, s32[]{:S(2)}) async-start(s8[5242880]{0:T(1024)(128)(4,1)} %bitcast.158), calls=%async_computation.1 | async-start | bytes 8388608
  602.2 8.1 %slice-start.1 = ((s8[5242880]{0:T(1024)(128)(4,1)}), s8[1048576]{0:T(1024)(128)(4,1)S(1)}, s32[]{:S(2)}) async-start(s8[5242880]{0:T(1024)(128)(4,1)} %bitcast.158), calls=%async_computation.2 | async-start | bytes 2097152
  618.7 8.1 %copy-start.9 = (bf16[640,4096]{1,0:T(8,128)(2,1)S(1)}, bf16[640,4096]{1,0:T(8,128)(2,1)}, u32[]{:S(2)}) copy-start(bf16[640,4096]{1,0:T(8,128)(2,1)} %copy-done.8) | copy-start | bytes 15728644
where the time goes:
time: 649 us; the launch traced here: 639 us
  matrix products  234 us (36%)
  blocking collectives  185 us (29%)
  local copies, waits for them, and re-layouts  119 us (18%)
  other arithmetic  80.3 us (12%)
  waiting for transfers between devices  15.8 us (2%)
    all_to_all x1, blocking collectives, shards(): lax.all_to_all(outgoing, 'bins', split_axis=2, concat_axis=1, tiled=True)  185 us
    dot_general x6, matrix products, complex_product(): jnp.einsum(form, left_real, right_imag, preferred_element_type=jnp.float32)  93.1 us
    dot_general x6, matrix products, complex_product(): jnp.einsum(form, left_real, right_real, preferred_element_type=jnp.float32)  51.5 us
    dot_general x6, matrix products, complex_product(): jnp.einsum(form, left_imag, right_imag, preferred_element_type=jnp.float32)  39.7 us
    dot_general x1, other arithmetic, migrate(): jnp.einsum('sprj,rjk->sprk', windows, band_matrix, preferred_element_type...  38.2 us
    dot_general x6, matrix products, complex_product(): jnp.einsum(form, left_imag, right_real, preferred_element_type=jnp.float32)  37.1 us
    convert_element_type x2, local copies, waits for them, and re-layouts, migrate(): return result.reshape(2, row_count, line_width).astype(jnp.bfloat16)  26.1 us
    concatenate x1, local copies, waits for them, and re-layouts, migrate(): jnp.concatenate([extended[:, :, :line_width].reshape(2, row_count, blocks...  23.6 us
  transfers between devices with their start and end apart: 1, of which 1 were waited for; matrix products, arithmetic and copies ran while one was open for 1% of the time, Pallas kernels for 0%

commit v1 on v0

v1 whole, which is shorter than its diff:
```python
import functools
import math

import jax
import jax.numpy as jnp
import numpy as np
from jax import lax
from jax.experimental import pallas as pl
from jax.experimental.pallas import tpu as pltpu
from jax.sharding import PartitionSpec as P

OVLMAX = 128
LANES = 128
CHUNK = 16
GROUP = 512
TILE = 256
EARLY_DIVISOR = 4
MESH = pl.DeviceIdType.MESH

COS_POLY = (
    1.0,
    -19.739208221435547,
    64.93939208984375,
    -85.45665740966797,
    60.242130279541016,
    -26.4046688079834,
    7.800131320953369,
    -1.453112244606018,
)
SIN_POLY = (
    6.2831854820251465,
    -41.34170150756836,
    81.6052474975586,
    -76.70580291748047,
    42.05775451660156,
    -15.086565017700195,
    3.7813189029693604,
    -0.6207787394523621,
)


def cosine_table(rows, cols, length):
    angle = 2.0 * math.pi / length * ((np.arange(rows)[:, None] * np.arange(cols)[None, :]) % length)
    return np.cos(angle), np.sin(angle)


def unit_turn(turns):
    r = turns - jnp.round(turns)
    s = r * r
    cosine = jnp.full_like(s, COS_POLY[-1])
    for value in COS_POLY[-2::-1]:
        cosine = cosine * s + value
    sine = jnp.full_like(s, SIN_POLY[-1])
    for value in SIN_POLY[-2::-1]:
        sine = sine * s + value
    return cosine, sine * r


def mm(left, right):
    return jnp.dot(left, right, preferred_element_type=jnp.float32)


def send_order(count):
    return sorted(range(1, count), key=lambda step: abs(2 * step - count))


def focus_kernel(
    n_bins,
    n_az,
    raw,
    filt,
    starts,
    weights,
    lengths,
    rates,
    dft,
    twiddle,
    az_table,
    out,
    raw_buf,
    xs,
    os_,
    send,
    recv,
    heads,
    ap,
    sp,
    out_buf,
    raw_sem,
    out_sem,
    early_send,
    early_recv,
    early_local,
    late_send,
    late_recv,
    late_local,
    head_send,
    head_recv,
):
    line = raw.shape[2]
    own = raw.shape[1]
    cols = out.shape[2]
    lines = out.shape[1]
    length = lines + OVLMAX
    chunks = own // CHUNK
    groups = cols // GROUP
    early = max(1, groups // EARLY_DIVISOR)
    early_width = early * GROUP + LANES
    me = lax.axis_index("bins")
    az = lax.axis_index("az")
    has_prev = az > 0
    has_next = az < n_az - 1
    order = send_order(n_bins)
    radix = line // LANES

    barrier = pltpu.get_barrier_semaphore()
    for step in range(1, n_bins):
        peer = lax.rem(me + step, n_bins)
        pl.semaphore_signal(barrier, inc=1, device_id={"bins": peer}, device_id_type=MESH)

    @pl.when(has_prev)
    def _():
        pl.semaphore_signal(barrier, inc=1, device_id={"az": az - 1}, device_id_type=MESH)

    @pl.when(has_next)
    def _():
        pl.semaphore_signal(barrier, inc=1, device_id={"az": az + 1}, device_id_type=MESH)

    def raw_copy(chunk, slot):
        return pltpu.make_async_copy(
            raw.at[:, pl.ds(pl.multiple_of(chunk * CHUNK, CHUNK), CHUNK), :], raw_buf.at[slot], raw_sem.at[slot]
        )

    raw_copy(0, 0).start()
    send[:, :, pl.ds(line, LANES)] = jnp.zeros((2, own, LANES), jnp.bfloat16)

    @pl.when(jnp.logical_not(has_next))
    def _():
        heads[...] = jnp.zeros(heads.shape, jnp.bfloat16)

    def early_copy(chunk, step, index):
        rows = pl.multiple_of(chunk * CHUNK, CHUNK)
        peer = lax.rem(me + step, n_bins)
        return pltpu.make_async_remote_copy(
            src_ref=send.at[:, pl.ds(rows, CHUNK), pl.ds(pl.multiple_of(peer * cols, LANES), early_width)],
            dst_ref=recv.at[:, pl.ds(pl.multiple_of(me * own + rows, CHUNK), CHUNK), pl.ds(0, early_width)],
            send_sem=early_send.at[chunk, index],
            recv_sem=early_recv.at[chunk, index],
            device_id={"bins": peer},
            device_id_type=MESH,
        )

    def early_own(chunk):
        rows = pl.multiple_of(chunk * CHUNK, CHUNK)
        return pltpu.make_async_copy(
            send.at[:, pl.ds(rows, CHUNK), pl.ds(pl.multiple_of(me * cols, LANES), early_width)],
            recv.at[:, pl.ds(pl.multiple_of(me * own + rows, CHUNK), CHUNK), pl.ds(0, early_width)],
            early_local.at[chunk],
        )

    def late_copy(group, step, index):
        peer = lax.rem(me + step, n_bins)
        first = group * GROUP + LANES
        return pltpu.make_async_remote_copy(
            src_ref=send.at[:, :, pl.ds(pl.multiple_of(peer * cols + first, LANES), GROUP)],
            dst_ref=recv.at[:, pl.ds(pl.multiple_of(me * own, CHUNK), own), pl.ds(pl.multiple_of(first, LANES), GROUP)],
            send_sem=late_send.at[group, index],
            recv_sem=late_recv.at[group, index],
            device_id={"bins": peer},
            device_id_type=MESH,
        )

    def late_own(group):
        first = group * GROUP + LANES
        return pltpu.make_async_copy(
            send.at[:, :, pl.ds(pl.multiple_of(me * cols + first, LANES), GROUP)],
            recv.at[:, pl.ds(pl.multiple_of(me * own, CHUNK), own), pl.ds(pl.multiple_of(first, LANES), GROUP)],
            late_local.at[group],
        )

    def head_copy(group, first, width):
        span = pl.ds(first, width)
        return pltpu.make_async_remote_copy(
            src_ref=recv.at[:, pl.ds(0, OVLMAX), span],
            dst_ref=heads.at[:, :, span],
            send_sem=head_send.at[group],
            recv_sem=head_recv.at[group],
            device_id={"az": az - 1},
            device_id_type=MESH,
        )

    def late_first(group):
        return pl.multiple_of(group * GROUP + LANES, LANES)

    def compress(chunk, carry):
        slot = lax.rem(chunk, 2)
        raw_copy(chunk, slot).wait()

        @pl.when(chunk + 1 < chunks)
        def _():
            raw_copy(chunk + 1, 1 - slot).start()

        def spread(index, inner):
            span = pl.ds(pl.multiple_of(index * LANES, LANES), LANES)
            for part in range(2):
                xs[part, pl.ds(index, CHUNK, radix), :] = raw_buf[slot, part, :, span].astype(jnp.float32)
            return inner

        lax.fori_loop(0, radix, spread, 0, unroll=8)

        def pulses(pair, inner):
            columns = []
            for which in range(2):
                rows = pl.ds(pl.multiple_of((2 * pair + which) * radix, radix), radix)
                columns.append(
                    jnp.concatenate([xs[0, rows, :], xs[1, rows, :]], axis=0).astype(jnp.bfloat16)
                )
            first = mm(dft[0], jnp.concatenate(columns, axis=1))
            tc, ts = twiddle[0], twiddle[1]
            stacked = []
            for which in range(2):
                re = first[:radix, which * LANES : (which + 1) * LANES]
                im = first[radix:, which * LANES : (which + 1) * LANES]
                stacked.append(
                    jnp.concatenate([re * tc + im * ts, im * tc - re * ts], axis=1).astype(jnp.bfloat16)
                )
            spectrum = mm(jnp.concatenate(stacked, axis=0), dft[1])
            fc, fs = filt[0], filt[1]
            stacked = []
            for which in range(2):
                re = spectrum[which * radix : (which + 1) * radix, :LANES]
                im = spectrum[which * radix : (which + 1) * radix, LANES:]
                stacked.append(
                    jnp.concatenate([re * fc + im * fs, im * fc - re * fs], axis=1).astype(jnp.bfloat16)
                )
            back = mm(jnp.concatenate(stacked, axis=0), dft[2])
            columns = []
            for which in range(2):
                re = back[which * radix : (which + 1) * radix, :LANES]
                im = back[which * radix : (which + 1) * radix, LANES:]
                columns.append(
                    jnp.concatenate([re * tc - im * ts, im * tc + re * ts], axis=0).astype(jnp.bfloat16)
                )
            last = mm(dft[3], jnp.concatenate(columns, axis=1))
            for which in range(2):
                for part in range(2):
                    os_[part, pl.ds(2 * pair + which, radix, CHUNK), :] = last[
                        part * radix : (part + 1) * radix, which * LANES : (which + 1) * LANES
                    ]
            return inner

        lax.fori_loop(0, CHUNK // 2, pulses, 0)
        rows_out = pl.ds(pl.multiple_of(chunk * CHUNK, CHUNK), CHUNK)

        def gather(index, inner):
            span = pl.ds(pl.multiple_of(index * LANES, LANES), LANES)
            rows = pl.ds(pl.multiple_of(index * CHUNK, CHUNK), CHUNK)
            for part in range(2):
                send[part, rows_out, span] = os_[part, rows, :].astype(jnp.bfloat16)
            return inner

        lax.fori_loop(0, radix, gather, 0, unroll=8)

        @pl.when(chunk == 0)
        def _():
            pl.semaphore_wait(barrier, n_bins - 1 + has_prev.astype(jnp.int32) + has_next.astype(jnp.int32))

        for index, step in enumerate(order):
            early_copy(chunk, step, index).start()
        early_own(chunk).start()
        return carry

    lax.fori_loop(0, chunks, compress, 0)

    def send_late(group, carry):
        for index, step in enumerate(order):
            late_copy(group, step, index).start()
        late_own(group).start()
        return carry

    lax.fori_loop(early, groups, send_late, 0)

    def out_copy(group, slot):
        return pltpu.make_async_copy(
            out_buf.at[slot],
            out.at[:, :, pl.ds(pl.multiple_of(group * GROUP, GROUP), GROUP)],
            out_sem.at[slot],
        )

    def focus(group, carry):
        @pl.when(group == 0)
        def _():
            def arrived(chunk, inner):
                for index, step in enumerate(order):
                    early_copy(chunk, step, index).wait_recv()
                early_own(chunk).wait()
                return inner

            lax.fori_loop(0, chunks, arrived, 0)

            @pl.when(has_prev)
            def _():
                head_copy(0, 0, early_width).start()

            @pl.when(has_next)
            def _():
                head_copy(0, 0, early_width).wait_recv()

        @pl.when(group >= early)
        def _():
            late_own(group).wait()
            for index, step in enumerate(order):
                late_copy(group, step, index).wait_recv()

            @pl.when(has_prev)
            def _():
                head_copy(group, late_first(group), GROUP).start()

            @pl.when(has_next)
            def _():
                head_copy(group, late_first(group), GROUP).wait_recv()

        slot = lax.rem(group, 2)

        @pl.when(group >= 2)
        def _():
            out_copy(group - 2, slot).wait()

        def tile(index, inner):
            for block in range(TILE // LANES):
                base = pl.multiple_of(group * GROUP + index * TILE + block * LANES, LANES)
                whole = pl.ds(pl.multiple_of(me * cols + base, LANES), LANES)
                offset = starts[:, whole] - (me * cols + base)
                taps = weights[:, whole].astype(jnp.float32)
                place = lax.broadcasted_iota(jnp.int32, (2 * LANES, LANES), 0) - offset
                band = jnp.zeros((2 * LANES, LANES), jnp.float32)
                for tap in range(taps.shape[0]):
                    band = jnp.where(place == tap, taps[tap : tap + 1, :], band)
                band = band.astype(jnp.bfloat16)
                inside = lax.broadcasted_iota(jnp.int32, (OVLMAX, LANES), 0) < lengths[:, pl.ds(base, LANES)]
                window = pl.ds(base, 2 * LANES)
                here = pl.ds(block * LANES, LANES)
                for part in range(2):
                    ap[part, pl.ds(0, lines), here] = mm(recv[part, :, window], band).astype(jnp.bfloat16)
                    tail = jnp.where(inside, mm(heads[part, :, window], band), 0.0)
                    ap[part, pl.ds(lines, OVLMAX), here] = tail.astype(jnp.bfloat16)
            re, im = ap[0], ap[1]
            spec_re = mm(az_table[:, : 2 * length], jnp.concatenate([re, -im], axis=0))
            spec_im = mm(az_table[:, length:], jnp.concatenate([re, im], axis=0))
            span = pl.ds(pl.multiple_of(group * GROUP + index * TILE, TILE), TILE)
            doppler = lax.broadcasted_iota(jnp.int32, (length, TILE), 0)
            signed = jnp.where(2 * doppler >= length, doppler - length, doppler)
            square = (signed * signed).astype(jnp.float32)
            fc, fs = unit_turn(square * (rates[:, span] * (0.5 / length)))
            sp[0] = (spec_re * fc + spec_im * fs).astype(jnp.bfloat16)
            sp[1] = (spec_im * fc - spec_re * fs).astype(jnp.bfloat16)
            re, im = sp[0], sp[1]
            here = pl.ds(pl.multiple_of(index * TILE, TILE), TILE)
            image = mm(az_table[:lines, : 2 * length], jnp.concatenate([re, im], axis=0))
            out_buf[slot, 0, :, here] = (image * (1.0 / length)).astype(jnp.bfloat16)
            image = mm(az_table[:lines, length:], jnp.concatenate([-re, im], axis=0))
            out_buf[slot, 1, :, here] = (image * (1.0 / length)).astype(jnp.bfloat16)
            return inner

        lax.fori_loop(0, GROUP // TILE, tile, 0)
        out_copy(group, slot).start()
        return carry

    lax.fori_loop(0, groups, focus, 0)
    for group in range(max(0, groups - 2), groups):
        out_copy(group, group % 2).wait()

    def early_done(chunk, carry):
        for index, step in enumerate(order):
            early_copy(chunk, step, index).wait_send()
        return carry

    lax.fori_loop(0, chunks, early_done, 0)

    def late_done(group, carry):
        for index, step in enumerate(order):
            late_copy(group, step, index).wait_send()

        @pl.when(has_prev)
        def _():
            head_copy(group, late_first(group), GROUP).wait_send()

        return carry

    lax.fori_loop(early, groups, late_done, 0)

    @pl.when(has_prev)
    def _():
        head_copy(0, 0, early_width).wait_send()


def shards(n_bins, n_az, raw_echoes, range_phase, band_start, band_weight, intersection_length, azimuth_rate):
    raw = raw_echoes[:, 0]
    own, line = raw.shape[1], raw.shape[2]
    cols = intersection_length.shape[0]
    lines = own * n_bins
    length = lines + OVLMAX
    radix = line // LANES
    groups = cols // GROUP
    chunks = own // CHUNK
    early_width = max(1, groups // EARLY_DIVISOR) * GROUP + LANES

    fr, fi = cosine_table(radix, radix, radix)
    fi = -fi
    dft = np.stack(
        [
            np.block([[fr, -fi], [fi, fr]]),
            np.block([[fr, fi], [-fi, fr]]),
            np.block([[fr, -fi], [fi, fr]]),
            np.block([[fr, fi], [-fi, fr]]) / line,
        ]
    )
    twiddle = np.stack(cosine_table(radix, LANES, line)).astype(np.float32)
    ar, ai = cosine_table(length, length, length)
    az_table = np.concatenate([ar, -ai, ar], axis=1)
    angle = range_phase.reshape(LANES, radix).T
    filt = jnp.stack([jnp.cos(angle), jnp.sin(angle)])

    vmem = pl.BlockSpec(memory_space=pltpu.VMEM)
    hbm = pl.BlockSpec(memory_space=pl.ANY)
    dma = pltpu.SemaphoreType.DMA
    bf16, f32 = jnp.bfloat16, jnp.float32
    image = pl.pallas_call(
        functools.partial(focus_kernel, n_bins, n_az),
        out_shape=jax.ShapeDtypeStruct((2, lines, cols), bf16),
        in_specs=[hbm] + [vmem] * 8,
        out_specs=hbm,
        scratch_shapes=[
            pltpu.VMEM((2, 2, CHUNK, line), bf16),
            pltpu.VMEM((2, CHUNK * radix, LANES), f32),
            pltpu.VMEM((2, CHUNK * radix, LANES), f32),
            pltpu.VMEM((2, own, line + LANES), bf16),
            pltpu.VMEM((2, lines, cols + LANES), bf16),
            pltpu.VMEM((2, OVLMAX, cols + LANES), bf16),
            pltpu.VMEM((2, length, TILE), bf16),
            pltpu.VMEM((2, length, TILE), bf16),
            pltpu.VMEM((2, 2, lines, GROUP), bf16),
            dma((2,)),
            dma((2,)),
            dma((chunks, n_bins - 1)),
            dma((chunks, n_bins - 1)),
            dma((chunks,)),
            dma((groups, n_bins - 1)),
            dma((groups, n_bins - 1)),
            dma((groups,)),
            dma((groups,)),
            dma((groups,)),
        ],
        compiler_params=pltpu.CompilerParams(
            collective_id=0, has_side_effects=True, vmem_limit_bytes=60 * 1024 * 1024
        ),
    )(
        raw,
        filt,
        band_start.reshape(1, line),
        band_weight,
        intersection_length.reshape(1, cols),
        azimuth_rate.reshape(1, cols),
        jnp.asarray(dft, bf16),
        jnp.asarray(twiddle),
        jnp.asarray(az_table, bf16),
    )
    return image[:, None]


def solution(mesh):
    in_specs = (P(None, ("scene", "az"), "bins", None), P(), P(), P(), P("bins"), P("bins"))
    out_specs = P(None, ("scene", "az"), None, "bins")
    body = functools.partial(shards, mesh.shape["bins"], mesh.shape["az"])
    return jax.shard_map(body, mesh=mesh, in_specs=in_specs, out_specs=out_specs, check_vma=False)
```

time: 649 us -> 237 us (0.37); the launches traced: 639 us -> 237 us
  matrix products: 234 us -> 0 us
  Pallas kernels: 0 us -> 227 us
  blocking collectives: 185 us -> 0 us
  local copies, waits for them, and re-layouts: 119 us -> 9.15 us
  other arithmetic: 80.3 us -> 0.67 us
  waiting for transfers between devices: 15.8 us -> 0 us
    dot_general x25 -> x0, matrix products: 234 us -> none  [the longest x6 93.1 us: complex_product(): jnp.einsum(form, left_real, right_imag, preferred_element_type=jnp.float32)]
    pallas_call x0 -> x1, Pallas kernels: none -> 227 us  [shards(): pl.pallas_call(functools.partial(focus_kernel, n_bins, n_az), out_shape=j...]
    all_to_all x1 -> x0, blocking collectives: 185 us -> none  [shards(): lax.all_to_all(outgoing, 'bins', split_axis=2, concat_axis=1, tiled=True)]
    dot_general x1 -> x0, other arithmetic: 38.2 us -> none  [migrate(): jnp.einsum('sprj,rjk->sprk', windows, band_matrix, preferred_element_type...]
    convert_element_type x2 -> x0, local copies, waits for them, and re-layouts: 26.1 us -> none  [migrate(): return result.reshape(2, row_count, line_width).astype(jnp.bfloat16)]
    convert_element_type x4 -> x0, other arithmetic: 24.4 us -> none  [the longest x2 13.8 us: compress_lines(): return stacked.reshape(2, line_count, line_width).astype(jnp.bfloat16)]
    concatenate x1 -> x0, local copies, waits for them, and re-layouts: 23.6 us -> none  [migrate(): jnp.concatenate([extended[:, :, :line_width].reshape(2, row_count, blocks...]
    all_to_all x2 -> x0, local copies, waits for them, and re-layouts: 22.6 us -> none  [shards(): lax.all_to_all(outgoing, 'bins', split_axis=2, concat_axis=1, tiled=True)]
  transfers between devices with their start and end apart: 1 -> 0, of which waited for: 1 -> 0; matrix products, arithmetic and copies ran while one was open for 1% -> 0% of each run, Pallas kernels for 0% -> 0%
where the time goes in v1:
time: 237 us
  Pallas kernels  227 us (96%)
  local copies, waits for them, and re-layouts  9.15 us (4%)
    pallas_call x1, Pallas kernels, shards(): pl.pallas_call(functools.partial(focus_kernel, n_bins, n_az), out_shape=j...  227 us
    unnamed x1, local copies, waits for them, and re-layouts  7.89 us

profile of v1, /device:TPU:9, one launch (start us, length us, event | category | flops | bytes accessed | tf_op | source)
XLA Modules:
  0.0 236.9 jit_solution(8224067977890593906)
XLA Ops:
  0.0 1.1 cosine_bitcast_fusion
  1.1 0.1 copy.11
  1.2 0.1 copy.12
  1.3 0.7 pad_maximum_fusion.filt
  1.9 227.1 %shard_map.91 = bf16[2,512,4096]{2,1,0:T(8,128)(2,1)} custom-call(bf16[2,128,16384]{2,1,0:T(8,128)(2,1)} %bitcast.18, f32[2,128,128]{2,1,0:T(8,128)} %pad_maximum_fusion.filt, s32[1,16384]{1,0:T(1,128)} %bitcast.21, bf16[8,16384]{1,0:T(8,128)(2,1)} %weights.1, s32[1,4096]{1,0:T(1,128)} %bitcast.22, f32[1,4096]{1,0:T(1,128)} %bitcast.23, ...), custom_call_target="tpu_custom_call" | custom-call | tf_op jit(solution)/shard_map/pallas_call | solution.py:428
  229.0 7.9 %copy.15 = bf16[2,1,512,4096]{3,2,1,0:T(8,128)(2,1)} copy(bf16[2,1,512,4096]{3,2,1,0:T(8,128)(2,1)} %bitcast.17) | data formatting | bytes 16777216

commit v2 on v1

--- a/solution.py
+++ b/solution.py
@@ -12,9 +12,9 @@
 OVLMAX = 128
 LANES = 128
 CHUNK = 16
-GROUP = 512
+GROUP = 256
 TILE = 256
-EARLY_DIVISOR = 4
+EARLY_SHARE = 5 / 16
 MESH = pl.DeviceIdType.MESH
 
 COS_POLY = (
@@ -104,7 +104,7 @@
     length = lines + OVLMAX
     chunks = own // CHUNK
     groups = cols // GROUP
-    early = max(1, groups // EARLY_DIVISOR)
+    early = max(1, int(groups * EARLY_SHARE))
     early_width = early * GROUP + LANES
     me = lax.axis_index("bins")
     az = lax.axis_index("az")
@@ -249,7 +249,7 @@
                     ]
             return inner
 
-        lax.fori_loop(0, CHUNK // 2, pulses, 0)
+        lax.fori_loop(0, CHUNK // 2, pulses, 0, unroll=4)
         rows_out = pl.ds(pl.multiple_of(chunk * CHUNK, CHUNK), CHUNK)
 
         def gather(index, inner):
@@ -403,7 +403,6 @@
     radix = line // LANES
     groups = cols // GROUP
     chunks = own // CHUNK
-    early_width = max(1, groups // EARLY_DIVISOR) * GROUP + LANES
 
     fr, fi = cosine_table(radix, radix, radix)
     fi = -fi

time: 237 us -> 218 us (0.920)
  Pallas kernels: 227 us -> 208 us
    pallas_call x1, Pallas kernels: 227 us -> 208 us  [shards(): pl.pallas_call(functools.partial(focus_kernel, n_bins, n_az), out_shape=j...]
where the time goes in v2:
time: 218 us
  Pallas kernels  208 us (95%)
  local copies, waits for them, and re-layouts  9.15 us (4%)
    pallas_call x1, Pallas kernels, shards(): pl.pallas_call(functools.partial(focus_kernel, n_bins, n_az), out_shape=j...  208 us
    unnamed x1, local copies, waits for them, and re-layouts  7.89 us

profile of v2, /device:TPU:9, one launch (start us, length us, event | category | flops | bytes accessed | tf_op | source)
XLA Modules:
  0.0 217.6 jit_solution(11517572713570140856)
XLA Ops:
  0.0 1.1 cosine_bitcast_fusion
  1.1 0.1 copy.11
  1.2 0.1 copy.12
  1.3 0.7 pad_maximum_fusion.filt
  1.9 207.8 %shard_map.91 = bf16[2,512,4096]{2,1,0:T(8,128)(2,1)} custom-call(bf16[2,128,16384]{2,1,0:T(8,128)(2,1)} %bitcast.18, f32[2,128,128]{2,1,0:T(8,128)} %pad_maximum_fusion.filt, s32[1,16384]{1,0:T(1,128)} %bitcast.21, bf16[8,16384]{1,0:T(8,128)(2,1)} %weights.1, s32[1,4096]{1,0:T(1,128)} %bitcast.22, f32[1,4096]{1,0:T(1,128)} %bitcast.23, ...), custom_call_target="tpu_custom_call" | custom-call | tf_op jit(solution)/shard_map/pallas_call | solution.py:427
  209.7 7.9 %copy.15 = bf16[2,1,512,4096]{3,2,1,0:T(8,128)(2,1)} copy(bf16[2,1,512,4096]{3,2,1,0:T(8,128)(2,1)} %bitcast.17) | data formatting | bytes 16777216
